TPU v7x, 32 devices: a whole 2x2x4 slice. The times are simulated.
32 devices in a mesh: fsdp: 4 (over x, core), ctx: 2 (over y), tp: 4 (over z).
Axes of the slice: x: 2, y: 2, z: 4, core: 2. Of those that a mesh axis runs over, the one named last changes fastest.
Arguments:
- tokens: bfloat16 [8, 1024, 768], P('fsdp', 'ctx'), may hold values from -6 to 6
- ln1_gain: float32 [768], replicated, may hold values from 0.1 to 1.9
- ln1_bias: float32 [768], replicated, may hold values from -1.75 to 1.75
- qkv_weight: bfloat16 [3, 768, 768], P(None, 'fsdp', 'tp'), may hold values from -0.21875 to 0.21875
- qv_bias: float32 [2, 768], P(None, 'tp'), may hold values from -1.25 to 1.25
- out_weight: bfloat16 [768, 768], P('tp', 'fsdp'), may hold values from -1.25 to 1.25
- out_bias: float32 [768], replicated, may hold values from -1.75 to 1.75
- ln2_gain: float32 [768], replicated, may hold values from 0.1 to 1.9
- ln2_bias: float32 [768], replicated, may hold values from -1.75 to 1.75
- fc_weight: bfloat16 [768, 3072], P('fsdp', 'tp'), may hold values from -0.21875 to 0.21875
- fc_bias: float32 [3072], P('tp'), may hold values from -3 to 3
- proj_weight: bfloat16 [3072, 768], P('tp', 'fsdp'), may hold values from -0.109375 to 0.109375
- proj_bias: float32 [768], replicated, may hold values from -1.75 to 1.75
- block_order: int32 [4], replicated, may hold values from 0 to 3, as said below
- out_grad: bfloat16 [8, 1024, 768], P('fsdp', 'ctx'), may hold values from -6 to 6
Outputs:
- result: bfloat16 [8, 1024, 768], P('fsdp', 'ctx')
- tokens_grad: float32 [8, 1024, 768], P('fsdp', 'ctx')
- ln1_gain_grad: float32 [768], replicated
- ln1_bias_grad: float32 [768], replicated
- qkv_weight_grad: float32 [3, 768, 768], P(None, 'fsdp', 'tp')
- qv_bias_grad: float32 [2, 768], P(None, 'tp')
- out_weight_grad: float32 [768, 768], P('tp', 'fsdp')
- out_bias_grad: float32 [768], replicated
- ln2_gain_grad: float32 [768], replicated
- ln2_bias_grad: float32 [768], replicated
- fc_weight_grad: float32 [768, 3072], P('fsdp', 'tp')
- fc_bias_grad: float32 [3072], P('tp')
- proj_weight_grad: float32 [3072, 768], P('tp', 'fsdp')
- proj_bias_grad: float32 [768], replicated
Inputs may be any that keep to these rules, and one draw needn't show every extreme that they name: block_order is a permutation of the 4 block numbers.
All inputs are finite; a program needn't handle non-finite values.
Results may differ from a plain program's by a relative error of at most 0.0099.
Values may be sent and summed in bfloat16 or wider, within the bound.
A program may use at most 192 MiB of HBM per device.

v0:
```python
import jax
import jax.numpy as jnp
from jax import lax
from jax.sharding import PartitionSpec as P

HD = 64


def gelu_curve(values):
    return jax.nn.gelu(values, approximate=True)


def normalized(values):
    centre = jnp.mean(values, axis=-1, keepdims=True)
    centred = values - centre
    scale = lax.rsqrt(jnp.mean(centred * centred, axis=-1, keepdims=True) + 1e-05)
    return (centred * scale, scale)


def norm_back(grad_in, gain, normed, scale):
    scaled = grad_in * gain
    return scale * (
        scaled
        - jnp.mean(scaled, axis=-1, keepdims=True)
        - normed * jnp.mean(scaled * normed, axis=-1, keepdims=True)
    )


def query_side(query_rows, pair_rows, grad_rows, lse_rows, visible):
    columns = query_rows.shape[1]
    heads_here = columns // HD
    length = pair_rows.shape[0]
    query_grad = jnp.zeros(query_rows.shape, jnp.float32)
    delta_cols = jnp.zeros((query_rows.shape[0], heads_here), jnp.float32)
    pair_term = jnp.zeros((length, 2 * columns), jnp.float32)

    def one_head(head_index, running):
        query_grad, pair_term, delta_cols = running
        start = head_index * HD
        query_head = lax.dynamic_slice_in_dim(query_rows, start, HD, 1)
        key_head = lax.dynamic_slice_in_dim(pair_rows, start, HD, 1)
        value_head = lax.dynamic_slice_in_dim(pair_rows, columns + start, HD, 1)
        grad_head = lax.dynamic_slice_in_dim(grad_rows, start, HD, 1)
        lse_head = lax.dynamic_slice_in_dim(lse_rows, head_index, 1, 1)
        scores = (
            jnp.einsum("qd,kd->qk", query_head, key_head, preferred_element_type=jnp.float32)
            * 0.125
        )
        scores = jnp.where(visible, scores, -1e30)
        prob_rows = jnp.exp(scores - lse_head)
        prob_grad = jnp.einsum(
            "qd,kd->qk", grad_head, value_head, preferred_element_type=jnp.float32
        )
        row_delta = jnp.sum(prob_rows * prob_grad, axis=-1, keepdims=True)
        score_grad = (prob_rows * (prob_grad - row_delta)).astype(jnp.bfloat16)
        query_part = (
            jnp.einsum("qk,kd->qd", score_grad, key_head, preferred_element_type=jnp.float32)
            * 0.125
        )
        query_grad = lax.dynamic_update_slice_in_dim(query_grad, query_part, start, 1)
        delta_cols = lax.dynamic_update_slice_in_dim(delta_cols, row_delta, head_index, 1)
        key_part = (
            jnp.einsum("qk,qd->kd", score_grad, query_head, preferred_element_type=jnp.float32)
            * 0.125
        )
        value_part = jnp.einsum(
            "qk,qd->kd",
            prob_rows.astype(jnp.bfloat16),
            grad_head,
            preferred_element_type=jnp.float32,
        )
        pair_term = lax.dynamic_update_slice_in_dim(pair_term, key_part, start, 1)
        pair_term = lax.dynamic_update_slice_in_dim(pair_term, value_part, columns + start, 1)
        return (query_grad, pair_term, delta_cols)

    return lax.fori_loop(0, heads_here, one_head, (query_grad, pair_term, delta_cols))


def body(
    tokens,
    ln1_gain,
    ln1_bias,
    qkv_weight,
    qv_bias,
    out_weight,
    out_bias,
    ln2_gain,
    ln2_bias,
    fc_weight,
    fc_bias,
    proj_weight,
    proj_bias,
    block_order,
    out_grad,
):
    seq_count, seq_rows, model_width = tokens.shape
    ctx_count = lax.axis_size("ctx")
    length = seq_rows * ctx_count
    block_rows = length // (2 * ctx_count)
    all_rows = jnp.arange(length, dtype=jnp.int32)
    slot_ids = jnp.arange(2 * ctx_count, dtype=jnp.int32)
    owner = all_rows[:, None] // block_rows == slot_ids[None, :]
    place_all = (
        jnp.sum(jnp.where(owner, block_order[None, :], 0), axis=1) * block_rows
        + all_rows % block_rows
    )
    place_here = lax.dynamic_slice_in_dim(place_all, lax.axis_index("ctx") * seq_rows, seq_rows)
    visible = place_here[:, None] >= place_all[None, :]
    whole_qkv, whole_out, whole_fc, whole_proj = (
        lax.all_gather(qkv_weight, "fsdp", axis=1, tiled=True),
        lax.all_gather(out_weight, "fsdp", axis=1, tiled=True),
        lax.all_gather(fc_weight, "fsdp", axis=0, tiled=True),
        lax.all_gather(proj_weight, "fsdp", axis=1, tiled=True),
    )
    columns = whole_qkv.shape[-1]
    heads_here = columns // HD
    total_rows = seq_count * seq_rows
    inputs = tokens.reshape(total_rows, model_width).astype(jnp.float32)
    normed_one, scale_one = normalized(inputs)
    act_one = (normed_one * ln1_gain + ln1_bias).astype(jnp.bfloat16)
    proj_qkv = jnp.einsum("td,cdh->cth", act_one, whole_qkv, preferred_element_type=jnp.float32)
    query = (proj_qkv[0] + qv_bias[0]).astype(jnp.bfloat16)
    key = proj_qkv[1].astype(jnp.bfloat16)
    value = (proj_qkv[2] + qv_bias[1]).astype(jnp.bfloat16)
    key_value = jnp.concatenate([key, value], axis=1).reshape(seq_count, seq_rows, 2 * columns)
    pair_whole = lax.all_gather(key_value, "ctx", axis=1, tiled=True)
    query_three = query.reshape(seq_count, seq_rows, columns)
    anchor = jnp.zeros((), jnp.int32)

    def forward_item(counter, running):
        attended, log_sums = running
        sequence = counter // heads_here
        head_index = counter % heads_here
        query_head = lax.dynamic_slice(
            query_three, (sequence, anchor, head_index * HD), (1, seq_rows, HD)
        )[0]
        key_head = lax.dynamic_slice(
            pair_whole, (sequence, anchor, head_index * HD), (1, length, HD)
        )[0]
        value_head = lax.dynamic_slice(
            pair_whole, (sequence, anchor, columns + head_index * HD), (1, length, HD)
        )[0]
        scores = (
            jnp.einsum("qd,kd->qk", query_head, key_head, preferred_element_type=jnp.float32)
            * 0.125
        )
        scores = jnp.where(visible, scores, -1e30)
        row_top = jnp.max(scores, axis=-1, keepdims=True)
        weights = jnp.exp(scores - row_top)
        row_total = jnp.sum(weights, axis=-1, keepdims=True)
        prob_low = (weights / row_total).astype(jnp.bfloat16)
        out_head = jnp.einsum("qk,kd->qd", prob_low, value_head, preferred_element_type=jnp.float32)
        attended = lax.dynamic_update_slice(
            attended, out_head[None], (sequence, anchor, head_index * HD)
        )
        log_sums = lax.dynamic_update_slice(
            log_sums, (row_top + jnp.log(row_total))[None], (sequence, anchor, head_index)
        )
        return (attended, log_sums)

    attended, log_sums = lax.fori_loop(
        0,
        seq_count * heads_here,
        forward_item,
        (
            jnp.zeros((seq_count, seq_rows, columns), jnp.float32),
            jnp.zeros((seq_count, seq_rows, heads_here), jnp.float32),
        ),
    )
    mixed = attended.reshape(total_rows, columns).astype(jnp.bfloat16)
    attn_out = (
        lax.psum(jnp.dot(mixed, whole_out, preferred_element_type=jnp.float32), "tp") + out_bias
    )
    middle = inputs + attn_out
    normed_two, scale_two = normalized(middle)
    act_two = (normed_two * ln2_gain + ln2_bias).astype(jnp.bfloat16)
    hidden_pre = jnp.dot(act_two, whole_fc, preferred_element_type=jnp.float32) + fc_bias
    hidden_out, gelu_back = jax.vjp(gelu_curve, hidden_pre)
    hidden = hidden_out.astype(jnp.bfloat16)
    branch = (
        lax.psum(
            jnp.dot(hidden, whole_proj, preferred_element_type=jnp.float32).astype(jnp.bfloat16),
            "tp",
        ).astype(jnp.float32)
        + proj_bias
    )
    result = (middle + branch).astype(jnp.bfloat16).reshape(seq_count, seq_rows, model_width)
    upstream_low = out_grad.reshape(total_rows, model_width)
    upstream = upstream_low.astype(jnp.float32)
    proj_bias_grad = jnp.sum(upstream, axis=0)
    proj_grad = jnp.einsum("tf,td->fd", hidden, upstream_low, preferred_element_type=jnp.float32)
    hidden_grad = jnp.einsum(
        "td,fd->tf", upstream_low, whole_proj, preferred_element_type=jnp.float32
    )
    pre_grad = gelu_back(hidden_grad)[0].astype(jnp.bfloat16)
    fc_bias_grad = jnp.sum(pre_grad.astype(jnp.float32), axis=0)
    fc_grad = jnp.einsum("td,tf->df", act_two, pre_grad, preferred_element_type=jnp.float32)
    act_two_grad = lax.psum(
        jnp.einsum("tf,df->td", pre_grad, whole_fc, preferred_element_type=jnp.float32), "tp"
    )
    ln2_gain_grad = jnp.sum(act_two_grad * normed_two, axis=0)
    ln2_bias_grad = jnp.sum(act_two_grad, axis=0)
    middle_grad = upstream + norm_back(act_two_grad, ln2_gain, normed_two, scale_two)
    attn_grad = middle_grad.astype(jnp.bfloat16)
    out_bias_grad = jnp.sum(attn_grad.astype(jnp.float32), axis=0)
    out_grad_weight = jnp.einsum("th,td->hd", mixed, attn_grad, preferred_element_type=jnp.float32)
    mixed_grad = (
        jnp.einsum("td,hd->th", attn_grad, whole_out, preferred_element_type=jnp.float32)
        .astype(jnp.bfloat16)
        .reshape(seq_count, seq_rows, columns)
    )
    query_grads = []
    pair_grads = []
    for sequence in range(seq_count):
        query_grad, pair_term, delta_cols = query_side(
            query_three[sequence],
            pair_whole[sequence],
            mixed_grad[sequence],
            log_sums[sequence],
            visible,
        )
        pair_grad = lax.psum_scatter(pair_term, "ctx", scatter_dimension=0, tiled=True)
        query_grads.append(query_grad)
        pair_grads.append(pair_grad)
    query_grad_low = jnp.concatenate(query_grads, axis=0).astype(jnp.bfloat16)
    pair_low = jnp.concatenate(pair_grads, axis=0).astype(jnp.bfloat16)
    stacked = jnp.stack([query_grad_low, pair_low[:, :columns], pair_low[:, columns:]])
    qv_bias_grad = jnp.stack(
        [
            jnp.sum(stacked[0].astype(jnp.float32), axis=0),
            jnp.sum(stacked[2].astype(jnp.float32), axis=0),
        ]
    )
    qkv_grad = jnp.einsum("td,cth->cdh", act_one, stacked, preferred_element_type=jnp.float32)
    act_one_grad = lax.psum(
        jnp.einsum("cth,cdh->td", stacked, whole_qkv, preferred_element_type=jnp.float32), "tp"
    )
    ln1_gain_grad = jnp.sum(act_one_grad * normed_one, axis=0)
    ln1_bias_grad = jnp.sum(act_one_grad, axis=0)
    tokens_grad = (middle_grad + norm_back(act_one_grad, ln1_gain, normed_one, scale_one)).reshape(
        seq_count, seq_rows, model_width
    )
    shard_qkv, shard_out, shard_fc, shard_proj = (
        lax.psum_scatter(qkv_grad, "fsdp", scatter_dimension=1, tiled=True),
        lax.psum_scatter(out_grad_weight, "fsdp", scatter_dimension=1, tiled=True),
        lax.psum_scatter(fc_grad, "fsdp", scatter_dimension=0, tiled=True),
        lax.psum_scatter(proj_grad, "fsdp", scatter_dimension=1, tiled=True),
    )
    shard_qkv, shard_out, shard_fc, shard_proj = lax.psum(
        (shard_qkv, shard_out, shard_fc, shard_proj), "ctx"
    )
    small_sums = lax.psum(
        (
            ln1_gain_grad,
            ln1_bias_grad,
            qv_bias_grad,
            out_bias_grad,
            ln2_gain_grad,
            ln2_bias_grad,
            fc_bias_grad,
            proj_bias_grad,
        ),
        ("fsdp", "ctx"),
    )
    return (
        result,
        tokens_grad,
        small_sums[0],
        small_sums[1],
        shard_qkv,
        small_sums[2],
        shard_out,
        small_sums[3],
        small_sums[4],
        small_sums[5],
        shard_fc,
        small_sums[6],
        shard_proj,
        small_sums[7],
    )


def solution(mesh):
    in_specs = (
        P("fsdp", "ctx", None),
        P(),
        P(),
        P(None, "fsdp", "tp"),
        P(None, "tp"),
        P("tp", "fsdp"),
        P(),
        P(),
        P(),
        P("fsdp", "tp"),
        P("tp"),
        P("tp", "fsdp"),
        P(),
        P(),
        P("fsdp", "ctx", None),
    )
    out_specs = (
        P("fsdp", "ctx", None),
        P("fsdp", "ctx", None),
        P(),
        P(),
        P(None, "fsdp", "tp"),
        P(None, "tp"),
        P("tp", "fsdp"),
        P(),
        P(),
        P(),
        P("fsdp", "tp"),
        P("tp"),
        P("tp", "fsdp"),
        P(),
    )
    return jax.shard_map(body, mesh=mesh, in_specs=in_specs, out_specs=out_specs, check_vma=False)
```

profile of v0, /device:TPU:0, one launch (start us, length us, event | category | flops | bytes accessed | tf_op | source)
XLA Modules:
  0.0 816.6 jit_solution(1400386524486620718)
XLA Ops:
  8.1 1.8 convert_reduce_fusion
  10.9 14.3 %all_gather.15 = bf16[3,768,192]{2,0,1:T(4,128)(2,1)S(1)} all-gather(bf16[3,192,192]{2,0,1:T(4,128)(2,1)S(1)} %copy.100), channel_id=1, replica_groups=mesh['fsdp'=4,'ctx'=2,'tp'=4] {'fsdp'}, dimensions={1}, use_global_device_ids=true | all-gather | bytes 1105920 | tf_op jit(solution)/shard_map/all_gather | solution.py:110
  25.2 2.0 copy.101
  34.7 6.6 all_gather.17
  41.3 20.8 %all-gather.4.cloned.1.call-done = bf16[2,1024,384]{1,2,0:T(8,128)(2,1)} async-done(((bf16[2,512,384]{1,2,0:T(8,128)(2,1)}), bf16[2,1024,384]{1,2,0:T(8,128)(2,1)}) %all-gather.4.cloned.1.call-update) | async-done | bytes 1572880 | tf_op jit(solution)/shard_map/all_gather | solution.py:126
  62.1 1.9 copy.105
  64.1 12.1 %while.54 = (s32[]{:T(128)}, bf16[2,512,192]{1,2,0:T(8,128)(2,1)S(1)}, f32[2,512,3]{1,2,0:T(4,128)S(1)}, bf16[2,512,192]{2,1,0:T(8,128)(2,1)S(1)}, bf16[2,1024,3...) while((s32[]{:T(128)}, ...), condition=%wide.region_6.7_spmd.clone, body=%wide.region_3.6_spmd.clone.sunk | while | flops 138935840 | bytes 7109057 | solution.py:161
  77.0 2.3 fusion.101
  81.0 119.5 %all-reduce.8.cloned.1.call-done = f32[1024,768]{1,0:T(8,128)} async-done(((f32[1024,768]{1,0:T(8,128)}), f32[1024,768]{1,0:T(8,128)}) %all-reduce.8.cloned.1.call-update) | async-done | bytes 3145744 | tf_op jit(solution)/shard_map/psum | solution.py:172
  200.5 2.8 fusion.94
  204.0 1.7 add_convert_fusion.1
  205.8 4.8 fusion.102
  210.6 6.4 convert_reduce_fusion.2
  218.1 3.1 fusion.103
  221.3 5.5 convolution_convert_fusion
  230.0 2.3 copy.110
  232.3 2.3 copy.114
  235.9 105.6 %all-reduce.12.cloned.1.call-done = f32[1024,768]{1,0:T(8,128)} async-done(((f32[1024,768]{1,0:T(8,128)}), f32[1024,768]{1,0:T(8,128)}) %all-reduce.12.cloned.1.call-update) | async-done | bytes 3145744 | tf_op jit(solution)/shard_map/psum | solution.py:198
  341.5 3.7 multiply_reduce_fusion.2
  345.8 66.5 %all-reduce.10.cloned.1.call-done = bf16[1024,768]{1,0:T(8,128)(2,1)} async-done(((bf16[1024,768]{1,0:T(8,128)(2,1)}), bf16[1024,768]{1,0:T(8,128)(2,1)}) %all-reduce.10.cloned.1.call-update) | async-done | bytes 1572880 | tf_op jit(solution)/shard_map/psum | solution.py:181
  412.3 5.2 convert_reduce_fusion.3
  419.5 11.1 %while.55 = (s32[]{:T(128)}, bf16[512,192]{0,1:T(8,128)(2,1)S(1)}, f32[1024,384]{0,1:T(8,128)S(1)}, bf16[512,192]{0,1:T(8,128)(2,1)S(1)}, bf16[1024,384]{1,0:T(8...) while((s32[]{:T(128)}, bf16[512,192]{0,1:T(8,128)(2,1)S(1)}, ...), condition=%wide.region_16.17_spmd.clone, body=%wide.region_14.16_spmd.clone.sunk | while | flops 340884992 | bytes 17449256 | solution.py:76
  433.9 26.1 %while.56 = (s32[]{:T(128)}, bf16[512,192]{0,1:T(8,128)(2,1)}, f32[1024,384]{0,1:T(8,128)}, bf16[512,192]{0,1:T(8,128)(2,1)S(1)}, bf16[1024,384]{1,0:T(8,128)(2,...) while((s32[]{:T(128)}, bf16[512,192]{0,1:T(8,128)(2,1)}, ...), condition=%wide.region_19.20_spmd.clone, body=%wide.region_17.19_spmd.clone.sunk | while | flops 340884992 | bytes 19022176 | solution.py:76
  434.8 1.6 fusion.175
  436.4 2.0 multiply_reduce_fusion.10
  445.0 2.0 multiply_reduce_fusion.10
  453.6 2.0 multiply_reduce_fusion.10
  456.5 1.5 fusion.176
  460.1 2.6 convolution_bitcast_fusion.2
  464.1 21.4 %reduce-scatter.13.cloned.1.call-done = f32[512,384]{0,1:T(8,128)} async-done(((f32[1024,384]{0,1:T(8,128)}), f32[512,384]{0,1:T(8,128)}) %reduce-scatter.13.cloned.1.call-update) | async-done | bytes 786448 | tf_op jit(solution)/shard_map/reduce_scatter | solution.py:222
  488.5 2.3 fusion.71
  490.8 3.0 copy.119
  493.8 2.8 reshape.261
  496.9 5.8 fusion.92
  504.1 2.9 fusion.104
  508.5 3.1 convolution_bitcast_fusion.1
  511.7 1.7 copy.122
  513.4 30.8 %reduce-scatter.19.cloned.1.call-done = f32[192,576]{1,0:T(8,128)} async-done(((f32[768,576]{1,0:T(8,128)}), f32[192,576]{1,0:T(8,128)}) %reduce-scatter.19.cloned.1.call-update) | async-done | bytes 442384
  546.7 32.9 %reduce-scatter.17.cloned.1.call-done = f32[768,192]{0,1:T(8,128)} async-done(((f32[768,768]{0,1:T(8,128)}), f32[768,192]{0,1:T(8,128)}) %reduce-scatter.17.cloned.1.call-update) | async-done | bytes 589840 | tf_op jit(solution)/shard_map/reduce_scatter | solution.py:247
  579.6 35.2 %reduce-scatter.15.cloned.1.call-done = f32[192,768]{1,0:T(8,128)} async-done(((f32[768,768]{1,0:T(8,128)}), f32[192,768]{1,0:T(8,128)}) %reduce-scatter.15.cloned.1.call-update) | async-done | bytes 589840 | tf_op jit(solution)/shard_map/reduce_scatter | solution.py:246
  618.0 120.8 %all-reduce.14.cloned.1.call-done = f32[1024,768]{1,0:T(8,128)} async-done(((f32[1024,768]{1,0:T(8,128)}), f32[1024,768]{1,0:T(8,128)}) %all-reduce.14.cloned.1.call-update) | async-done | bytes 3145744 | tf_op jit(solution)/shard_map/psum | solution.py:235
  738.9 3.1 fusion.68
  742.0 25.4 %all-reduce = (f32[768]{0:T(1024)}, f32[768]{0:T(1024)}, f32[2,192]{1,0:T(2,128)}, f32[768]{0:T(1024)}, f32[768]{0:T(1024)}, /*index=5*/f32[768]{0:T(1024)}, f32[768]{0:T(1024)}, f32[768]{0:T(1024)}) all-reduce(f32[768]{0:T(1024)S(1)} %get-tuple-element.847, ...), channel_id=1, replica_groups=mesh['fsdp'=4,'ctx'=2,'tp'=4] {'fsdp','ctx'}, use_global_device_ids=true, to_apply=%region_26.27 | all-reduce | flops 5760 | bytes 46080 | tf_op jit(solution)/shard_map/psum | solution.py:252
  767.4 4.5 fusion.67
  772.0 30.4 %all-reduce.16.cloned.1.call-done = (f32[3,192,192]{1,2,0:T(8,128)}, f32[192,192]{1,0:T(8,128)}, f32[192,768]{1,0:T(8,128)}, f32[768,192]{0,1:T(8,128)}) async-done(((f32[3,192,192]{1,2,0:T(8,128)}, f32[192,192]{1,0:T(8,128)}, f32[192,768]{1,0:T(8,128)}, f32[768,192]{0,1:T(8,128)}), (f32[3,192,192]{1,2,0:T(8,128)}, f32[192,192]{1,0:T(8,128)}, f32[192,768]{1,0:T(8,128)}, ...) | async-done | bytes 1769488 | tf_op jit(solution)/shard_map/psum | solution.py:249
  802.4 2.2 copy.117
  804.6 1.6 copy.195
  806.2 1.9 copy.196
  (273 shorter events, 76.5 us)
Async XLA Ops:
  8.0 2.5 copy-start.31
  8.0 54.1 %all-gather.4.cloned.1.call-start = ((), (), s32[]{:S(2)}) async-start(), calls=%async_computation.6 | async-start | bytes 2359296 | tf_op jit(solution)/shard_map/all_gather | solution.py:126
  10.6 16.7 %copy-start.33 = (f32[1,4,2,128]{3,1,2,0:T(4,128)}, f32[1,4,2,128]{3,1,2,0:T(4,128)S(1)}, u32[]{:S(2)}) copy-start(f32[1,4,2,128]{3,1,2,0:T(4,128)S(1)} %copy.148) | copy-start | bytes 12292
  10.8 16.4 %copy-start.37 = (f32[768]{0:T(1024)S(1)}, f32[768]{0:T(1024)}, u32[]{:S(2)}) copy-start(f32[768]{0:T(1024)} %param.22) | copy-start | bytes 9220
  10.8 16.4 %copy-start.46 = (f32[768]{0:T(1024)S(1)}, f32[768]{0:T(1024)}, u32[]{:S(2)}) copy-start(f32[768]{0:T(1024)} %param.23) | copy-start | bytes 9220
  32.1 1.9 copy-start.32
  33.0 8.2 %copy-start.44 = (f32[1,192]{1,0:T(1,128)S(1)}, f32[1,192]{1,0:T(1,128)}, u32[]{:S(2)}) copy-start(f32[1,192]{1,0:T(1,128)} %get-tuple-element.943) | copy-start | bytes 2308
  33.9 166.5 %all-reduce.8.cloned.1.call-start = ((), (), s32[]{:S(2)}) async-start(), calls=%async_computation.7 | async-start | bytes 6291456 | tf_op jit(solution)/shard_map/psum | solution.py:172
  41.2 35.0 %copy-start.11 = (bf16[192,768]{0,1:T(8,128)(2,1)}, bf16[192,768]{0,1:T(8,128)(2,1)S(1)}, u32[]{:S(2)}) copy-start(bf16[192,768]{0,1:T(8,128)(2,1)S(1)} %all_gather.17) | copy-start | bytes 884740
  76.1 3.1 copy-start.35
  79.3 121.2 %copy-start.47 = (f32[768]{0:T(1024)S(1)}, f32[768]{0:T(1024)}, u32[]{:S(2)}) copy-start(f32[768]{0:T(1024)} %param.27) | copy-start | bytes 9220
  79.3 126.5 %all-gather.6.cloned.1.call-start = ((), (), s32[]{:S(2)}) async-start(), calls=%async_computation.8 | async-start | bytes 1474560 | tf_op jit(solution)/shard_map/all_gather | solution.py:112
  79.9 130.7 %all-gather.8.cloned.1.call-start = ((), (), s32[]{:S(2)}) async-start(), calls=%async_computation.9 | async-start | bytes 1474560 | tf_op jit(solution)/shard_map/all_gather | solution.py:113
  80.5 261.0 %all-reduce.12.cloned.1.call-start = ((), (), s32[]{:S(2)}) async-start(), calls=%async_computation.11 | async-start | bytes 6291456 | tf_op jit(solution)/shard_map/psum | solution.py:198
  205.8 4.8 copy-start.53
  210.6 7.6 copy-start.52
  221.3 191.0 %all-reduce.10.cloned.1.call-start = ((), (), s32[]{:S(2)}) async-start(), calls=%async_computation.10 | async-start | bytes 3145728 | tf_op jit(solution)/shard_map/psum | solution.py:181
  221.3 5.7 copy-start.45
  226.8 236.0 %reduce-scatter.11.cloned.1.call-start = ((), (), s32[]{:S(2)}) async-start(), calls=%async_computation.12 | async-start | bytes 2359296 | tf_op jit(solution)/shard_map/reduce_scatter | solution.py:222
  412.3 5.2 copy-start.12
  430.6 3.3 copy-start.23
  430.6 3.3 copy-start.8
  431.8 53.7 %reduce-scatter.13.cloned.1.call-start = ((), (), s32[]{:S(2)}) async-start(), calls=%async_computation.13 | async-start | bytes 2359296 | tf_op jit(solution)/shard_map/reduce_scatter | solution.py:222
  433.9 26.2 %copy-start.3 = (f32[1024,768]{1,0:T(8,128)S(1)}, f32[1024,768]{1,0:T(8,128)}, u32[]{:S(2)}) copy-start(f32[1024,768]{1,0:T(8,128)} %copy-done.2) | copy-start | bytes 9437188
  440.8 2.1 copy-start.20
  449.4 2.0 copy-start.20
  458.0 2.0 copy-start.20
  460.0 51.6 %reduce-scatter.21.cloned.1.call-start = ((), (), s32[]{:S(2)}) async-start(), calls=%async_computation.18 | async-start | bytes 983040
  462.7 25.7 %copy-start.15 = (bf16[1024,768]{1,0:T(8,128)(2,1)S(1)}, bf16[1024,768]{1,0:T(8,128)(2,1)}, u32[]{:S(2)}) copy-start(bf16[1024,768]{1,0:T(8,128)(2,1)} %copy-done.14) | copy-start | bytes 4718596
  462.7 25.7 %copy-start.21 = (bf16[512,192]{0,1:T(8,128)(2,1)S(1)}, bf16[512,192]{0,1:T(8,128)(2,1)}, u32[]{:S(2)}) copy-start(bf16[512,192]{0,1:T(8,128)(2,1)} %get-tuple-element.574) | copy-start | bytes 589828
  462.7 25.7 %copy-start.24 = (bf16[512,192]{0,1:T(8,128)(2,1)S(1)}, bf16[512,192]{0,1:T(8,128)(2,1)}, u32[]{:S(2)}) copy-start(bf16[512,192]{0,1:T(8,128)(2,1)} %copy-done.23) | copy-start | bytes 589828
  462.8 81.5 %reduce-scatter.19.cloned.1.call-start = ((), (), s32[]{:S(2)}) async-start(), calls=%async_computation.17 | async-start | bytes 2457600
  493.8 3.1 copy-start.54
  496.6 83.0 %reduce-scatter.17.cloned.1.call-start = ((), (), s32[]{:S(2)}) async-start(), calls=%async_computation.16 | async-start | bytes 2949120 | tf_op jit(solution)/shard_map/reduce_scatter | solution.py:247
  496.9 5.9 copy-start.56
  502.7 112.1 %reduce-scatter.15.cloned.1.call-start = ((), (), s32[]{:S(2)}) async-start(), calls=%async_computation.15 | async-start | bytes 2949120 | tf_op jit(solution)/shard_map/reduce_scatter | solution.py:246
  507.0 231.8 %all-reduce.14.cloned.1.call-start = ((), (), s32[]{:S(2)}) async-start(), calls=%async_computation.14 | async-start | bytes 6291456 | tf_op jit(solution)/shard_map/psum | solution.py:235
  511.6 290.8 %all-reduce.16.cloned.1.call-start = ((), (), s32[]{:S(2)}) async-start(), calls=%async_computation.19 | async-start | bytes 3932160 | tf_op jit(solution)/shard_map/psum | solution.py:249
  513.4 101.4 %copy-start.7 = (bf16[2,512,768]{2,1,0:T(8,128)(2,1)S(1)}, bf16[2,512,768]{2,1,0:T(8,128)(2,1)}, u32[]{:S(2)}) copy-start(bf16[2,512,768]{2,1,0:T(8,128)(2,1)} %param.35) | copy-start | bytes 4718596
  614.8 124.1 %copy-start.1 = (bf16[2,512,768]{2,1,0:T(8,128)(2,1)S(1)}, bf16[2,512,768]{2,1,0:T(8,128)(2,1)}, u32[]{:S(2)}) copy-start(bf16[2,512,768]{2,1,0:T(8,128)(2,1)} %param.21) | copy-start | bytes 4718596
  614.8 124.1 %copy-start.34 = (f32[1,4,2,128]{3,1,2,0:T(4,128)S(1)}, f32[1,4,2,128]{3,1,2,0:T(4,128)}, u32[]{:S(2)}) copy-start(f32[1,4,2,128]{3,1,2,0:T(4,128)} %copy-done.33) | copy-start | bytes 12292
  614.8 124.1 %copy-start.38 = (f32[768]{0:T(1024)S(1)}, f32[768]{0:T(1024)}, u32[]{:S(2)}) copy-start(f32[768]{0:T(1024)} %param.22) | copy-start | bytes 9220
  617.9 124.0 %copy-start.40 = (f32[768]{0:T(1024)S(1)}, f32[768]{0:T(1024)}, u32[]{:S(2)}) copy-start(f32[768]{0:T(1024)} %get-tuple-element.917) | copy-start | bytes 9220
  618.0 124.0 %copy-start.41 = (f32[768]{0:T(1024)S(1)}, f32[768]{0:T(1024)}, u32[]{:S(2)}) copy-start(f32[768]{0:T(1024)} %convert_reduce_fusion.1) | copy-start | bytes 9220
  618.0 124.0 %copy-start.42 = (f32[768]{0:T(1024)S(1)}, f32[768]{0:T(1024)}, u32[]{:S(2)}) copy-start(f32[768]{0:T(1024)} %get-tuple-element.845) | copy-start | bytes 9220
  618.0 124.0 %copy-start.43 = (f32[768]{0:T(1024)S(1)}, f32[768]{0:T(1024)}, u32[]{:S(2)}) copy-start(f32[768]{0:T(1024)} %get-tuple-element.851) | copy-start | bytes 9220
  618.0 124.0 %copy-start.49 = (f32[768]{0:T(1024)S(1)}, f32[768]{0:T(1024)}, u32[]{:S(2)}) copy-start(f32[768]{0:T(1024)} %get-tuple-element.915) | copy-start | bytes 9220
  802.4 5.7 copy-start.26
  (27 other events, 33.8 us)
Sparse Core Ops, SparseCore 0:
  34.1 28.0 all-gather.3
  79.4 121.0 all-reduce.7
  221.4 120.0 all-reduce.11
  344.3 67.9 all-reduce.9
  431.9 25.2 reduce-scatter.10
  460.2 25.3 reduce-scatter.12
  488.1 23.1 reduce-scatter.20
  513.9 30.3 reduce-scatter.18
  546.8 32.7 reduce-scatter.16
  582.0 32.7 reduce-scatter.14
  617.8 121.0 all-reduce.13
  742.3 60.0 all-reduce.15
Sparse Core Ops, SparseCore 1:
  81.3 17.3 all-gather.5
  100.1 17.3 all-gather.7
where the time goes:
time: 824 us; the launch traced here: 817 us
  waiting for transfers between devices  585 us (71%)
  matrix products  77.9 us (9%)
  local copies, waits for them, and re-layouts  50.1 us (6%)
  blocking collectives  46.3 us (6%)
  other arithmetic  38.2 us (5%)
  between operations  16.6 us (2%)
    psum x1, waiting for transfers between devices, body(): lax.psum(jnp.einsum('cth,cdh->td', stacked, whole_qkv, preferred_element_...  121 us
    psum x1, waiting for transfers between devices, body(): lax.psum(jnp.dot(mixed, whole_out, preferred_element_type=jnp.float32), '...  120 us
    psum x1, waiting for transfers between devices, body(): lax.psum(jnp.einsum('tf,df->td', pre_grad, whole_fc, preferred_element_ty...  106 us
    psum x1, waiting for transfers between devices, body(): lax.psum(jnp.dot(hidden, whole_proj, preferred_element_type=jnp.float32)....  66.5 us
    reduce_scatter x1, waiting for transfers between devices, body(): lax.psum_scatter(fc_grad, 'fsdp', scatter_dimension=0, tiled=True)  35.2 us
    unnamed x126, local copies, waits for them, and re-layouts  33.5 us
    reduce_scatter x1, waiting for transfers between devices, body(): lax.psum_scatter(proj_grad, 'fsdp', scatter_dimension=1, tiled=True)  32.9 us
    unnamed x16, waiting for transfers between devices  32.1 us
  transfers between devices with their start and end apart: 14, of which 10 were waited for; matrix products, arithmetic and copies ran while one was open for 12% of the time, Pallas kernels for 0%

commit v1 on v0

--- a/solution.py
+++ b/solution.py
@@ -178,9 +178,14 @@
     hidden_out, gelu_back = jax.vjp(gelu_curve, hidden_pre)
     hidden = hidden_out.astype(jnp.bfloat16)
     branch = (
-        lax.psum(
-            jnp.dot(hidden, whole_proj, preferred_element_type=jnp.float32).astype(jnp.bfloat16),
-            "tp",
+        jnp.sum(
+            lax.all_gather(
+                jnp.dot(hidden, whole_proj, preferred_element_type=jnp.float32).astype(
+                    jnp.bfloat16
+                ),
+                "tp",
+            ),
+            axis=0,
         ).astype(jnp.float32)
         + proj_bias
     )

time: 824 us -> 874 us (1.061)
  waiting for transfers between devices: 585 us -> 630 us
    all_gather x0 -> x1, waiting for transfers between devices: none -> 112 us  [body(): lax.all_gather(jnp.dot(hidden, whole_proj, preferred_element_type=jnp.flo...]
    psum x1 -> x0, waiting for transfers between devices: 66.5 us -> none  [body(): lax.psum(jnp.dot(hidden, whole_proj, preferred_element_type=jnp.float32)....]
  transfers between devices with their start and end apart: 14 -> 14, of which waited for: 10 -> 10; matrix products, arithmetic and copies ran while one was open for 12% -> 11% of each run, Pallas kernels for 0% -> 0%
where the time goes in v1:
time: 874 us; the launch traced here: 867 us
  waiting for transfers between devices  630 us (72%)
  matrix products  77.8 us (9%)
  local copies, waits for them, and re-layouts  50.1 us (6%)
  blocking collectives  46.3 us (5%)
  other arithmetic  43.5 us (5%)
  between operations  16.6 us (2%)
    psum x1, waiting for transfers between devices, body(): lax.psum(jnp.einsum('cth,cdh->td', stacked, whole_qkv, preferred_element_...  121 us
    psum x1, waiting for transfers between devices, body(): lax.psum(jnp.dot(mixed, whole_out, preferred_element_type=jnp.float32), '...  120 us
    all_gather x1, waiting for transfers between devices, body(): lax.all_gather(jnp.dot(hidden, whole_proj, preferred_element_type=jnp.flo...  112 us
    psum x1, waiting for transfers between devices, body(): lax.psum(jnp.einsum('tf,df->td', pre_grad, whole_fc, preferred_element_ty...  106 us
    reduce_scatter x1, waiting for transfers between devices, body(): lax.psum_scatter(fc_grad, 'fsdp', scatter_dimension=0, tiled=True)  35.2 us
    unnamed x126, local copies, waits for them, and re-layouts  33.4 us
    reduce_scatter x1, waiting for transfers between devices, body(): lax.psum_scatter(proj_grad, 'fsdp', scatter_dimension=1, tiled=True)  32.9 us
    unnamed x16, waiting for transfers between devices  32.3 us
  transfers between devices with their start and end apart: 14, of which 10 were waited for; matrix products, arithmetic and copies ran while one was open for 11% of the time, Pallas kernels for 0%

profile of v1, /device:TPU:0, one launch (start us, length us, event | category | flops | bytes accessed | tf_op | source)
XLA Modules:
  0.0 866.5 jit_solution(15454619980911746188)
XLA Ops:
  8.1 1.8 convert_reduce_fusion
  10.9 14.3 %all_gather.21 = bf16[3,768,192]{2,0,1:T(4,128)(2,1)S(1)} all-gather(bf16[3,192,192]{2,0,1:T(4,128)(2,1)S(1)} %copy.100), channel_id=1, replica_groups=mesh['fsdp'=4,'ctx'=2,'tp'=4] {'fsdp'}, dimensions={1}, use_global_device_ids=true | all-gather | bytes 1105920 | tf_op jit(solution)/shard_map/all_gather | solution.py:110
  25.2 2.0 copy.101
  34.6 6.6 all_gather.23
  41.2 20.8 %all-gather.6.cloned.1.call-done = bf16[2,1024,384]{1,2,0:T(8,128)(2,1)} async-done(((bf16[2,512,384]{1,2,0:T(8,128)(2,1)}), bf16[2,1024,384]{1,2,0:T(8,128)(2,1)}) %all-gather.6.cloned.1.call-update) | async-done | bytes 1572880 | tf_op jit(solution)/shard_map/all_gather | solution.py:126
  62.1 1.9 copy.105
  64.0 12.1 %while.54 = (s32[]{:T(128)}, bf16[2,512,192]{1,2,0:T(8,128)(2,1)S(1)}, f32[2,512,3]{1,2,0:T(4,128)S(1)}, bf16[2,512,192]{2,1,0:T(8,128)(2,1)S(1)}, bf16[2,1024,3...) while((s32[]{:T(128)}, ...), condition=%wide.region_6.7_spmd.clone, body=%wide.region_3.6_spmd.clone.sunk | while | flops 138935840 | bytes 7109057 | solution.py:161
  76.9 2.3 fusion.101
  80.9 119.5 %all-reduce.7.cloned.1.call-done = f32[1024,768]{1,0:T(8,128)} async-done(((f32[1024,768]{1,0:T(8,128)}), f32[1024,768]{1,0:T(8,128)}) %all-reduce.7.cloned.1.call-update) | async-done | bytes 3145744 | tf_op jit(solution)/shard_map/psum | solution.py:172
  200.4 2.8 fusion.94
  204.0 1.7 add_convert_fusion.1
  205.7 4.8 fusion.102
  210.5 6.4 convert_reduce_fusion.2
  218.0 3.1 fusion.103
  221.2 5.5 convolution_convert_fusion
  229.9 2.3 copy.110
  232.2 2.3 copy.114
  235.8 105.6 %all-reduce.9.cloned.1.call-done = f32[1024,768]{1,0:T(8,128)} async-done(((f32[1024,768]{1,0:T(8,128)}), f32[1024,768]{1,0:T(8,128)}) %all-reduce.9.cloned.1.call-update) | async-done | bytes 3145744 | tf_op jit(solution)/shard_map/psum | solution.py:203
  341.4 3.7 multiply_reduce_fusion.2
  345.6 112.1 %all-gather.12.cloned.1.call-done = bf16[4096,768]{1,0:T(8,128)(2,1)} async-done(((bf16[1024,768]{1,0:T(8,128)(2,1)}), bf16[4096,768]{1,0:T(8,128)(2,1)}) %all-gather.12.cloned.1.call-update) | async-done | bytes 6291472 | tf_op jit(solution)/shard_map/all_gather | solution.py:182
  457.7 5.3 reduce_sum.227
  463.0 5.2 convert_reduce_fusion.3
  470.2 11.1 %while.55 = (s32[]{:T(128)}, bf16[512,192]{0,1:T(8,128)(2,1)S(1)}, f32[1024,384]{0,1:T(8,128)S(1)}, bf16[512,192]{0,1:T(8,128)(2,1)S(1)}, bf16[1024,384]{1,0:T(8...) while((s32[]{:T(128)}, bf16[512,192]{0,1:T(8,128)(2,1)S(1)}, ...), condition=%wide.region_16.17_spmd.clone, body=%wide.region_14.16_spmd.clone.sunk | while | flops 340884992 | bytes 17449256 | solution.py:76
  484.7 26.1 %while.56 = (s32[]{:T(128)}, bf16[512,192]{0,1:T(8,128)(2,1)}, f32[1024,384]{0,1:T(8,128)}, bf16[512,192]{0,1:T(8,128)(2,1)S(1)}, bf16[1024,384]{1,0:T(8,128)(2,...) while((s32[]{:T(128)}, bf16[512,192]{0,1:T(8,128)(2,1)}, ...), condition=%wide.region_19.20_spmd.clone, body=%wide.region_17.19_spmd.clone.sunk | while | flops 340884992 | bytes 19022176 | solution.py:76
  485.5 1.6 fusion.175
  487.1 2.0 multiply_reduce_fusion.10
  495.7 2.0 multiply_reduce_fusion.10
  504.3 2.0 multiply_reduce_fusion.10
  510.8 2.6 convolution_bitcast_fusion.2
  515.1 20.3 %reduce-scatter.13.cloned.1.call-done = f32[512,384]{0,1:T(8,128)} async-done(((f32[1024,384]{0,1:T(8,128)}), f32[512,384]{0,1:T(8,128)}) %reduce-scatter.13.cloned.1.call-update) | async-done | bytes 786448 | tf_op jit(solution)/shard_map/reduce_scatter | solution.py:227
  538.3 2.3 fusion.71
  540.7 3.0 copy.119
  543.6 2.8 reshape.262
  546.6 5.8 fusion.92
  553.7 2.9 fusion.104
  558.1 3.1 convolution_bitcast_fusion.1
  561.3 1.7 copy.122
  563.0 31.1 %reduce-scatter.19.cloned.1.call-done = f32[192,576]{1,0:T(8,128)} async-done(((f32[768,576]{1,0:T(8,128)}), f32[192,576]{1,0:T(8,128)}) %reduce-scatter.19.cloned.1.call-update) | async-done | bytes 442384
  596.6 32.9 %reduce-scatter.17.cloned.1.call-done = f32[768,192]{0,1:T(8,128)} async-done(((f32[768,768]{0,1:T(8,128)}), f32[768,192]{0,1:T(8,128)}) %reduce-scatter.17.cloned.1.call-update) | async-done | bytes 589840 | tf_op jit(solution)/shard_map/reduce_scatter | solution.py:252
  629.5 35.2 %reduce-scatter.15.cloned.1.call-done = f32[192,768]{1,0:T(8,128)} async-done(((f32[768,768]{1,0:T(8,128)}), f32[192,768]{1,0:T(8,128)}) %reduce-scatter.15.cloned.1.call-update) | async-done | bytes 589840 | tf_op jit(solution)/shard_map/reduce_scatter | solution.py:251
  667.9 120.9 %all-reduce.11.cloned.1.call-done = f32[1024,768]{1,0:T(8,128)} async-done(((f32[1024,768]{1,0:T(8,128)}), f32[1024,768]{1,0:T(8,128)}) %all-reduce.11.cloned.1.call-update) | async-done | bytes 3145744 | tf_op jit(solution)/shard_map/psum | solution.py:240
  788.8 3.1 fusion.68
  791.9 25.4 %all-reduce = (f32[768]{0:T(1024)}, f32[768]{0:T(1024)}, f32[2,192]{1,0:T(2,128)}, f32[768]{0:T(1024)}, f32[768]{0:T(1024)}, /*index=5*/f32[768]{0:T(1024)}, f32[768]{0:T(1024)}, f32[768]{0:T(1024)}) all-reduce(f32[768]{0:T(1024)S(1)} %get-tuple-element.847, ...), channel_id=1, replica_groups=mesh['fsdp'=4,'ctx'=2,'tp'=4] {'fsdp','ctx'}, use_global_device_ids=true, to_apply=%region_26.27 | all-reduce | flops 5760 | bytes 46080 | tf_op jit(solution)/shard_map/psum | solution.py:257
  817.3 4.5 fusion.67
  821.9 30.4 %all-reduce.13.cloned.1.call-done = (f32[3,192,192]{1,2,0:T(8,128)}, f32[192,192]{1,0:T(8,128)}, f32[192,768]{1,0:T(8,128)}, f32[768,192]{0,1:T(8,128)}) async-done(((f32[3,192,192]{1,2,0:T(8,128)}, f32[192,192]{1,0:T(8,128)}, f32[192,768]{1,0:T(8,128)}, f32[768,192]{0,1:T(8,128)}), (f32[3,192,192]{1,2,0:T(8,128)}, f32[192,192]{1,0:T(8,128)}, f32[192,768]{1,0:T(8,128)}, ...) | async-done | bytes 1769488 | tf_op jit(solution)/shard_map/psum | solution.py:254
  852.3 2.2 copy.117
  854.5 1.6 copy.194
  856.1 1.9 copy.195
  (274 shorter events, 78.0 us)
Async XLA Ops:
  8.0 2.5 copy-start.31
  8.0 54.0 %all-gather.6.cloned.1.call-start = ((), (), s32[]{:S(2)}) async-start(), calls=%async_computation.6 | async-start | bytes 2359296 | tf_op jit(solution)/shard_map/all_gather | solution.py:126
  10.6 16.7 %copy-start.33 = (f32[1,4,2,128]{3,1,2,0:T(4,128)}, f32[1,4,2,128]{3,1,2,0:T(4,128)S(1)}, u32[]{:S(2)}) copy-start(f32[1,4,2,128]{3,1,2,0:T(4,128)S(1)} %copy.148) | copy-start | bytes 12292
  10.8 16.4 %copy-start.37 = (f32[768]{0:T(1024)S(1)}, f32[768]{0:T(1024)}, u32[]{:S(2)}) copy-start(f32[768]{0:T(1024)} %param.22) | copy-start | bytes 9220
  10.8 16.4 %copy-start.46 = (f32[768]{0:T(1024)S(1)}, f32[768]{0:T(1024)}, u32[]{:S(2)}) copy-start(f32[768]{0:T(1024)} %param.23) | copy-start | bytes 9220
  32.0 1.9 copy-start.32
  32.9 8.2 copy-start.44
  33.9 166.5 %all-reduce.7.cloned.1.call-start = ((), (), s32[]{:S(2)}) async-start(), calls=%async_computation.7 | async-start | bytes 6291456 | tf_op jit(solution)/shard_map/psum | solution.py:172
  41.1 35.0 %copy-start.11 = (bf16[192,768]{0,1:T(8,128)(2,1)}, bf16[192,768]{0,1:T(8,128)(2,1)S(1)}, u32[]{:S(2)}) copy-start(bf16[192,768]{0,1:T(8,128)(2,1)S(1)} %all_gather.23) | copy-start | bytes 884740
  76.1 3.1 copy-start.35
  79.2 121.2 %copy-start.47 = (f32[768]{0:T(1024)S(1)}, f32[768]{0:T(1024)}, u32[]{:S(2)}) copy-start(f32[768]{0:T(1024)} %param.27) | copy-start | bytes 9220
  79.2 126.5 %all-gather.8.cloned.1.call-start = ((), (), s32[]{:S(2)}) async-start(), calls=%async_computation.8 | async-start | bytes 1474560 | tf_op jit(solution)/shard_map/all_gather | solution.py:112
  79.8 130.7 %all-gather.10.cloned.1.call-start = ((), (), s32[]{:S(2)}) async-start(), calls=%async_computation.9 | async-start | bytes 1474560 | tf_op jit(solution)/shard_map/all_gather | solution.py:113
  80.4 261.0 %all-reduce.9.cloned.1.call-start = ((), (), s32[]{:S(2)}) async-start(), calls=%async_computation.10 | async-start | bytes 6291456 | tf_op jit(solution)/shard_map/psum | solution.py:203
  205.7 4.8 copy-start.53
  210.5 7.6 copy-start.52
  221.2 5.8 copy-start.45
  221.2 236.6 %all-gather.12.cloned.1.call-start = ((), (), s32[]{:S(2)}) async-start(), calls=%async_computation.16 | async-start | bytes 7864320 | tf_op jit(solution)/shard_map/all_gather | solution.py:182
  226.7 287.0 %reduce-scatter.11.cloned.1.call-start = ((), (), s32[]{:S(2)}) async-start(), calls=%async_computation.11 | async-start | bytes 2359296 | tf_op jit(solution)/shard_map/reduce_scatter | solution.py:227
  463.0 5.2 copy-start.12
  481.4 3.3 copy-start.23
  481.4 3.3 copy-start.8
  482.5 52.9 %reduce-scatter.13.cloned.1.call-start = ((), (), s32[]{:S(2)}) async-start(), calls=%async_computation.12 | async-start | bytes 2359296 | tf_op jit(solution)/shard_map/reduce_scatter | solution.py:227
  484.7 26.2 %copy-start.3 = (f32[1024,768]{1,0:T(8,128)S(1)}, f32[1024,768]{1,0:T(8,128)}, u32[]{:S(2)}) copy-start(f32[1024,768]{1,0:T(8,128)} %copy-done.2) | copy-start | bytes 9437188
  491.5 2.1 copy-start.20
  500.1 2.0 copy-start.20
  508.7 2.0 copy-start.20
  510.8 50.5 %reduce-scatter.21.cloned.1.call-start = ((), (), s32[]{:S(2)}) async-start(), calls=%async_computation.18 | async-start | bytes 983040
  513.4 24.9 %copy-start.15 = (bf16[1024,768]{1,0:T(8,128)(2,1)S(1)}, bf16[1024,768]{1,0:T(8,128)(2,1)}, u32[]{:S(2)}) copy-start(bf16[1024,768]{1,0:T(8,128)(2,1)} %copy-done.14) | copy-start | bytes 4718596
  513.4 24.9 %copy-start.21 = (bf16[512,192]{0,1:T(8,128)(2,1)S(1)}, bf16[512,192]{0,1:T(8,128)(2,1)}, u32[]{:S(2)}) copy-start(bf16[512,192]{0,1:T(8,128)(2,1)} %get-tuple-element.574) | copy-start | bytes 589828
  513.4 24.9 %copy-start.24 = (bf16[512,192]{0,1:T(8,128)(2,1)S(1)}, bf16[512,192]{0,1:T(8,128)(2,1)}, u32[]{:S(2)}) copy-start(bf16[512,192]{0,1:T(8,128)(2,1)} %copy-done.23) | copy-start | bytes 589828
  513.5 80.6 %reduce-scatter.19.cloned.1.call-start = ((), (), s32[]{:S(2)}) async-start(), calls=%async_computation.17 | async-start | bytes 2457600
  543.6 2.9 copy-start.54
  546.5 83.0 %reduce-scatter.17.cloned.1.call-start = ((), (), s32[]{:S(2)}) async-start(), calls=%async_computation.15 | async-start | bytes 2949120 | tf_op jit(solution)/shard_map/reduce_scatter | solution.py:252
  546.5 5.9 copy-start.56
  552.4 112.4 %reduce-scatter.15.cloned.1.call-start = ((), (), s32[]{:S(2)}) async-start(), calls=%async_computation.14 | async-start | bytes 2949120 | tf_op jit(solution)/shard_map/reduce_scatter | solution.py:251
  556.7 232.1 %all-reduce.11.cloned.1.call-start = ((), (), s32[]{:S(2)}) async-start(), calls=%async_computation.13 | async-start | bytes 6291456 | tf_op jit(solution)/shard_map/psum | solution.py:240
  561.3 291.1 %all-reduce.13.cloned.1.call-start = ((), (), s32[]{:S(2)}) async-start(), calls=%async_computation.19 | async-start | bytes 3932160 | tf_op jit(solution)/shard_map/psum | solution.py:254
  563.0 101.7 %copy-start.7 = (bf16[2,512,768]{2,1,0:T(8,128)(2,1)S(1)}, bf16[2,512,768]{2,1,0:T(8,128)(2,1)}, u32[]{:S(2)}) copy-start(bf16[2,512,768]{2,1,0:T(8,128)(2,1)} %param.35) | copy-start | bytes 4718596
  664.7 124.1 %copy-start.1 = (bf16[2,512,768]{2,1,0:T(8,128)(2,1)S(1)}, bf16[2,512,768]{2,1,0:T(8,128)(2,1)}, u32[]{:S(2)}) copy-start(bf16[2,512,768]{2,1,0:T(8,128)(2,1)} %param.21) | copy-start | bytes 4718596
  664.7 124.1 %copy-start.34 = (f32[1,4,2,128]{3,1,2,0:T(4,128)S(1)}, f32[1,4,2,128]{3,1,2,0:T(4,128)}, u32[]{:S(2)}) copy-start(f32[1,4,2,128]{3,1,2,0:T(4,128)} %copy-done.33) | copy-start | bytes 12292
  664.7 124.1 %copy-start.38 = (f32[768]{0:T(1024)S(1)}, f32[768]{0:T(1024)}, u32[]{:S(2)}) copy-start(f32[768]{0:T(1024)} %param.22) | copy-start | bytes 9220
  667.9 124.0 %copy-start.40 = (f32[768]{0:T(1024)S(1)}, f32[768]{0:T(1024)}, u32[]{:S(2)}) copy-start(f32[768]{0:T(1024)} %get-tuple-element.917) | copy-start | bytes 9220
  667.9 124.0 %copy-start.41 = (f32[768]{0:T(1024)S(1)}, f32[768]{0:T(1024)}, u32[]{:S(2)}) copy-start(f32[768]{0:T(1024)} %convert_reduce_fusion.1) | copy-start | bytes 9220
  667.9 124.0 %copy-start.42 = (f32[768]{0:T(1024)S(1)}, f32[768]{0:T(1024)}, u32[]{:S(2)}) copy-start(f32[768]{0:T(1024)} %get-tuple-element.845) | copy-start | bytes 9220
  667.9 124.0 %copy-start.43 = (f32[768]{0:T(1024)S(1)}, f32[768]{0:T(1024)}, u32[]{:S(2)}) copy-start(f32[768]{0:T(1024)} %get-tuple-element.851) | copy-start | bytes 9220
  667.9 124.0 %copy-start.49 = (f32[768]{0:T(1024)S(1)}, f32[768]{0:T(1024)}, u32[]{:S(2)}) copy-start(f32[768]{0:T(1024)} %get-tuple-element.915) | copy-start | bytes 9220
  852.3 5.7 copy-start.26
  (27 other events, 33.7 us)
Sparse Core Ops, SparseCore 0:
  34.0 28.0 all-gather.5
  79.3 121.0 all-reduce.6
  221.3 120.0 all-reduce.8
  343.4 114.3 all-gather.11
  482.6 24.3 reduce-scatter.10
  510.9 24.4 reduce-scatter.12
  537.9 23.1 reduce-scatter.20
  563.7 30.3 reduce-scatter.18
  596.7 32.8 reduce-scatter.16
  631.9 32.8 reduce-scatter.14
  667.7 121.0 all-reduce.10
  792.3 60.0 all-reduce.12
Sparse Core Ops, SparseCore 1:
  81.2 17.3 all-gather.7
  100.0 17.3 all-gather.9
